TPU v7x, 128 devices: a whole 4x4x4 slice. The times are simulated.
128 devices in a mesh: sx: 8 (over y_hi, x), sy: 8 (over z, core), par: 2 (over y_lo).
Axes of the slice: x: 4, y: 4 (y_hi: 2, y_lo: 2; y = y_hi * 2 + y_lo), z: 4, core: 2. Of those that a mesh axis runs over, the one named last changes fastest.
Arguments:
- initial_state: float32 [64, 128, 128, 128], P('par', 'sx', 'sy'), may hold values from -6 to 6
- conductivity: float32 [64, 128, 128, 128], P('par', 'sx', 'sy'), may hold values from 0.1 to 1
- omega: bfloat16 [64, 64], replicated, may hold values from -0.75 to 0.75
- psi: bfloat16 [64, 128, 128, 128], P(None, 'sx', 'sy'), may hold values from -0.01171875 to 0.01171875
- range_prev: bfloat16 [64, 128, 128, 128], P('par', 'sx', 'sy'), may hold values from -3 to 3
- corange_prev: float32 [64, 64], P(None, 'par'), may hold values from -3 to 3
Outputs:
- final_state: float32 [64, 128, 128, 128], P('par', 'sx', 'sy')
- range_sketch: bfloat16 [64, 128, 128, 128], P('par', 'sx', 'sy')
- corange_sketch: float32 [64, 64], P(None, 'par')
All inputs are finite; a program needn't handle non-finite values.
Results may differ from a plain program's by a relative error of at most 0.0033.
Values may be sent and summed in bfloat16 or wider, within the bound.
A program may use at most 192 MiB of HBM per device.

v0:
```python
import jax
import jax.numpy as jnp
from jax import lax
from jax.sharding import PartitionSpec as P

STEPS = 4


def extended(block, sides, width):
    for axis, dim in sides:
        count = lax.axis_size(axis)
        forward = [(i, i + 1) for i in range(count - 1)]
        backward = [(target, source) for source, target in forward]
        low = lax.ppermute(
            lax.slice_in_dim(block, block.shape[dim] - width, None, axis=dim), axis, forward
        )
        high = lax.ppermute(lax.slice_in_dim(block, 0, width, axis=dim), axis, backward)
        block = jnp.concatenate([low, block, high], axis=dim)
    return block


def advance(field, kpad):
    center = field[:, 1:-1, 1:-1, :]
    kcen = kpad[:, 1:-1, 1:-1, :]
    width_x = center.shape[1]
    width_y = center.shape[2]
    zfield = jnp.pad(center, ((0, 0), (0, 0), (0, 0), (1, 1)))
    zcond = jnp.pad(kcen, ((0, 0), (0, 0), (0, 0), (1, 1)))
    length = center.shape[3]
    pairs = [
        (field[:, 2:, 1:-1, :], kpad[:, 2:, 1:-1, :]),
        (field[:, :width_x, 1:-1, :], kpad[:, :width_x, 1:-1, :]),
        (field[:, 1:-1, 2:, :], kpad[:, 1:-1, 2:, :]),
        (field[:, 1:-1, :width_y, :], kpad[:, 1:-1, :width_y, :]),
        (zfield[:, :, :, 2:], zcond[:, :, :, 2:]),
        (zfield[:, :, :, :length], zcond[:, :, :, :length]),
    ]
    total = jnp.zeros_like(center)
    for unb, knb in pairs:
        total = total + 0.5 * (kcen + knb) * (unb - center)
    return center + 0.16 * total


def per_device(initial_state, conductivity, omega, psi, range_prev, corange_prev):
    samples, cells_x, cells_y, length = initial_state.shape
    kpad = extended(conductivity, (("sx", 1), ("sy", 2)), 1)
    state = initial_state
    for step in range(STEPS):
        field = extended(state, (("sx", 1), ("sy", 2)), 1)
        state = advance(field, kpad)
    snapshot = state.astype(jnp.bfloat16)
    flat_snap = snapshot.reshape(samples, cells_x * cells_y * length)
    rank = omega.shape[1]
    rank_dev = range_prev.shape[0]
    own_cols = lax.dynamic_slice_in_dim(omega, lax.axis_index("par") * rank_dev, rank_dev, 1)
    start_sum = range_prev.astype(jnp.float32)
    piece = lax.all_gather(snapshot, "par", axis=0, tiled=True)
    rows = piece.shape[0]
    term = lax.dot_general(
        own_cols,
        piece.reshape(rows, -1),
        (((0,), (0,)), ((), ())),
        preferred_element_type=jnp.float32,
    )
    range_sum = start_sum + term.reshape(start_sum.shape)
    range_sketch = range_sum.astype(jnp.bfloat16)
    flat_psi = psi.reshape(rank, cells_x * cells_y * length)
    partial_value = lax.dot_general(
        flat_psi, flat_snap, (((1,), (1,)), ((), ())), preferred_element_type=jnp.float32
    )
    corange_sketch = corange_prev + lax.psum(partial_value, ("sx", "sy"))
    return (state, range_sketch, corange_sketch)


def solution(mesh):
    in_specs = (
        P("par", "sx", "sy", None),
        P("par", "sx", "sy", None),
        P(),
        P(None, "sx", "sy", None),
        P("par", "sx", "sy", None),
        P(None, "par"),
    )
    out_specs = (P("par", "sx", "sy", None), P("par", "sx", "sy", None), P(None, "par"))
    return jax.shard_map(
        per_device, mesh=mesh, in_specs=in_specs, out_specs=out_specs, check_vma=False
    )
```

profile of v0, /device:TPU:24, one launch (start us, length us, event | category | flops | bytes accessed | tf_op | source)
XLA Modules:
  0.0 525.8 jit_solution(14510973290693297946)
XLA Ops:
  7.2 4.8 copy.22
  12.0 3.4 collective-permute-start.2
  15.5 6.3 %collective-permute-start = (f32[32,1,16,128]{3,0,2,1:T(8,128)S(1)}, f32[32,1,16,128]{3,0,2,1:T(8,128)S(1)}, u32[]{:S(2)}, u32[]{:S(2)}) collective-permute-start(f32[32,1,16,128]{3,0,2,1:T(8,128)S(1)} %get-tuple-element.31), channel_id=1, source_target_pairs={{16,0},{32,16},{48,32},{64,48},{80,64},{96,80},{112,96},{17,1},{33... | collective-permute-start | bytes 786440 | tf_op jit(solution)/shard_map/ppermute | solution.py:17
  21.8 2.4 copy.44
  24.3 1.9 collective-permute-start.3
  26.2 7.5 %collective-permute-start.1 = (f32[32,1,16,128]{3,0,2,1:T(8,128)S(1)}, f32[32,1,16,128]{3,0,2,1:T(8,128)S(1)}, u32[]{:S(2)}, u32[]{:S(2)}) collective-permute-start(f32[32,1,16,128]{3,0,2,1:T(8,128)S(1)} %get-tuple-element.32), channel_id=1, source_target_pairs={{16,0},{32,16},{48,32},{64,48},{80,64},{96,80},{112,96},{17,1},{33... | collective-permute-start | bytes 786440 | tf_op jit(solution)/shard_map/ppermute | solution.py:17
  33.8 2.4 constant_dynamic-update-slice_fusion.1
  36.3 1.3 collective-permute-start.4
  37.6 3.0 collective-permute-start.6
  41.4 4.4 constant_dynamic-update-slice_fusion.4
  45.8 0.7 constant_dynamic-update-slice_fusion.3
  46.5 1.1 fusion.103
  47.6 1.3 collective-permute-start.5
  48.9 4.3 collective-permute-start.7
  53.2 1.0 collective-permute-done.7
  54.2 10.3 %fusion.9 = f32[32,16,16,128]{3,0,2,1:T(8,128)S(1)} fusion(f32[32,16,16,128]{3,0,2,1:T(8,128)S(1)} %copy.44, f32[32,18,16,128]{3,0,2,1:T(8,128)} %constant_dynamic-update-slice_fusion.3, f32[32,18,1,128]{3,0,2,1:T(8,128)S(1)} %collective-permute-done.7, f32[32,18,1,128]{3,0,2,1:T(8,128)S(1)} %collective-permute-done.5, ...), kind=kLoop, calls=%fused_computation.19 | loop fusion | flops 40894464 | bytes 24248320 | tf_op jit(solution)/shard_map/add | solution.py:41
  64.5 1.9 collective-permute-start.8
  66.5 3.9 collective-permute-start.9
  70.4 2.4 collective-permute-done.8
  72.8 5.5 %collective-permute-done.9 = f32[32,1,16,128]{3,0,2,1:T(8,128)S(1)} collective-permute-done((f32[32,1,16,128]{3,0,2,1:T(8,128)S(1)}, f32[32,1,16,128]{3,0,2,1:T(8,128)S(1)}, u32[]{:S(2)}, u32[]{:S(2)}) %collective-permute-start.9) | collective-permute-done | bytes 262176 | tf_op jit(solution)/shard_map/ppermute | solution.py:14
  78.4 1.3 collective-permute-start.10
  79.7 5.6 %collective-permute-start.11 = (f32[32,18,1,128]{3,0,2,1:T(8,128)S(1)}, f32[32,18,1,128]{3,0,2,1:T(8,128)S(1)}, u32[]{:S(2)}, u32[]{:S(2)}) collective-permute-start(f32[32,18,1,128]{3,0,2,1:T(8,128)S(1)} %get-tuple-element.19), channel_id=1, source_target_pairs={{0,2},{2,4},{4,6},{6,8},{8,10},{10,12},{12,14},{1,3},{3,5},{5,7},{... | collective-permute-start | bytes 884744 | tf_op jit(solution)/shard_map/ppermute | solution.py:14
  85.3 1.2 collective-permute-done.11
  86.5 8.1 %fusion.17 = f32[32,16,16,128]{3,0,2,1:T(8,128)S(1)} fusion(f32[32,16,16,128]{3,0,2,1:T(8,128)S(1)} %fusion.9, f32[32,18,1,128]{3,0,2,1:T(8,128)S(1)} %collective-permute-done.11, f32[32,1,16,128]{3,0,2,1:T(8,128)S(1)} %collective-permute-done.8, f32[32,1,16,128]{3,0,2,1:T(8,128)S(1)} %collective-permute-done.9, ...), kind=kLoop, calls=%fused_computation.27 | loop fusion | flops 45088768 | bytes 19529728 | tf_op jit(solution)/shard_map/add | solution.py:41
  94.6 1.9 collective-permute-start.12
  96.5 3.9 collective-permute-start.13
  100.5 2.4 collective-permute-done.12
  102.9 5.5 %collective-permute-done.13 = f32[32,1,16,128]{3,0,2,1:T(8,128)S(1)} collective-permute-done((f32[32,1,16,128]{3,0,2,1:T(8,128)S(1)}, f32[32,1,16,128]{3,0,2,1:T(8,128)S(1)}, u32[]{:S(2)}, u32[]{:S(2)}) %collective-permute-start.13) | collective-permute-done | bytes 262176 | tf_op jit(solution)/shard_map/ppermute | solution.py:14
  108.5 1.3 collective-permute-start.14
  109.8 8.9 %collective-permute-start.15 = (f32[32,18,1,128]{3,0,2,1:T(8,128)S(1)}, f32[32,18,1,128]{3,0,2,1:T(8,128)S(1)}, u32[]{:S(2)}, u32[]{:S(2)}) collective-permute-start(f32[32,18,1,128]{3,0,2,1:T(8,128)S(1)} %get-tuple-element.17), channel_id=1, source_target_pairs={{0,2},{2,4},{4,6},{6,8},{8,10},{10,12},{12,14},{1,3},{3,5},{5,7},{... | collective-permute-start | bytes 884744 | tf_op jit(solution)/shard_map/ppermute | solution.py:14
  118.7 1.2 collective-permute-done.15
  119.8 8.1 %fusion.25 = f32[32,16,16,128]{3,0,2,1:T(8,128)S(1)} fusion(f32[32,16,16,128]{3,0,2,1:T(8,128)S(1)} %fusion.17, f32[32,18,1,128]{3,0,2,1:T(8,128)S(1)} %collective-permute-done.15, f32[32,1,16,128]{3,0,2,1:T(8,128)S(1)} %collective-permute-done.12, f32[32,1,16,128]{3,0,2,1:T(8,128)S(1)} %collective-permute-done.13, ...), kind=kLoop, calls=%fused_computation.35 | loop fusion | flops 45088768 | bytes 19529728 | tf_op jit(solution)/shard_map/add | solution.py:41
  128.0 1.9 collective-permute-start.16
  129.9 3.9 collective-permute-start.17
  133.8 2.4 collective-permute-done.16
  136.2 5.5 %collective-permute-done.17 = f32[32,1,16,128]{3,0,2,1:T(8,128)S(1)} collective-permute-done((f32[32,1,16,128]{3,0,2,1:T(8,128)S(1)}, f32[32,1,16,128]{3,0,2,1:T(8,128)S(1)}, u32[]{:S(2)}, u32[]{:S(2)}) %collective-permute-start.17) | collective-permute-done | bytes 262176 | tf_op jit(solution)/shard_map/ppermute | solution.py:14
  141.8 1.3 collective-permute-start.18
  143.1 8.6 %collective-permute-start.19 = (f32[32,18,1,128]{3,0,2,1:T(8,128)S(1)}, f32[32,18,1,128]{3,0,2,1:T(8,128)S(1)}, u32[]{:S(2)}, u32[]{:S(2)}) collective-permute-start(f32[32,18,1,128]{3,0,2,1:T(8,128)S(1)} %get-tuple-element.15), channel_id=1, source_target_pairs={{0,2},{2,4},{4,6},{6,8},{8,10},{10,12},{12,14},{1,3},{3,5},{5,7},{... | collective-permute-start | bytes 884744 | tf_op jit(solution)/shard_map/ppermute | solution.py:14
  151.7 1.2 collective-permute-done.19
  152.9 9.7 %fusion.100 = (bf16[32,16,16,128]{3,0,2,1:T(8,128)(2,1)S(1)}, f32[32,16,16,128]{3,0,2,1:T(8,128)}) fusion(f32[32,16,16,128]{3,0,2,1:T(8,128)S(1)} %fusion.25, f32[32,16,16,128]{3,0,2,1:T(8,128)S(1)} %copy.22, f32[32,1,16,128]{3,0,2,1:T(8,128)S(1)} %collective-permute-done.16, f32[32,1,16,128]{3,0,2,1:T(8,128)S(1)} %collective-permute-done.17, ...), kind=kLoop, calls=%fused_computation.155 | loop fusion | flops 46137344 | bytes 21626880 | tf_op jit(solution)/shard_map/convert_element_type | solution.py:51
  162.6 2.1 copy.47
  164.8 6.8 %copy.50 = f32[32,16,16,128]{3,2,1,0:T(8,128)} copy(f32[32,16,16,128]{3,0,2,1:T(8,128)} %get-tuple-element.13) | data formatting | bytes 8388608
  171.6 3.7 fusion.94
  175.3 330.3 %psum.7 = f32[64,32]{0,1:T(8,128)S(1)} all-reduce(f32[64,32]{0,1:T(8,128)S(1)} %fusion.94), channel_id=1, replica_groups=mesh['sx'=8,'sy'=8,'par'=2] {'sx','sy'}, use_global_device_ids=true, to_apply=%region_0.1 | all-reduce | flops 2048 | bytes 16384 | tf_op jit(solution)/shard_map/psum | solution.py:71
  506.2 4.9 copy.69
  511.2 1.2 copy.56
  512.7 4.1 add_convert_fusion
  516.8 2.1 copy.51
  (38 shorter events, 2.2 us)
Async XLA Ops:
  7.2 505.2 %copy-start = (bf16[64,64]{1,0:T(8,128)(2,1)S(1)}, bf16[64,64]{1,0:T(8,128)(2,1)}, u32[]{:S(2)}) copy-start(bf16[64,64]{1,0:T(8,128)(2,1)} %param.8) | copy-start | bytes 24580
  7.2 499.1 %all-gather.2.cloned.1.call-start = ((), (), s32[]{:S(2)}) async-start(), calls=%async_computation | async-start | bytes 6291456 | tf_op jit(solution)/shard_map/all_gather | solution.py:57
  7.2 14.6 %copy-start.2 = (f32[32,16,16,128]{3,2,1,0:T(8,128)S(1)}, f32[32,16,16,128]{3,2,1,0:T(8,128)}, u32[]{:S(2)}) copy-start(f32[32,16,16,128]{3,2,1,0:T(8,128)} %param.6) | copy-start | bytes 12582916
  12.0 21.7 %collective-permute-start.2 = (f32[32,1,16,128]{3,0,2,1:T(8,128)S(1)}, f32[32,1,16,128]{3,0,2,1:T(8,128)S(1)}, u32[]{:S(2)}, u32[]{:S(2)}) collective-permute-start(f32[32,1,16,128]{3,0,2,1:T(8,128)S(1)} %get-tuple-element.30), channel_id=1, source_target_pairs={{0,16},{16,32},{32,48},{48,64},{64,80},{80,96},{96,112},{1,17},{17... | collective-permute-start | bytes 786440 | tf_op jit(solution)/shard_map/ppermute | solution.py:14
  15.5 18.3 %copy-start.1 = (f32[32,16,16,128]{3,2,1,0:T(8,128)S(1)}, f32[32,16,16,128]{3,2,1,0:T(8,128)}, u32[]{:S(2)}) copy-start(f32[32,16,16,128]{3,2,1,0:T(8,128)} %param.7) | copy-start | bytes 12582916
  15.5 20.8 %collective-permute-start = (f32[32,1,16,128]{3,0,2,1:T(8,128)S(1)}, f32[32,1,16,128]{3,0,2,1:T(8,128)S(1)}, u32[]{:S(2)}, u32[]{:S(2)}) collective-permute-start(f32[32,1,16,128]{3,0,2,1:T(8,128)S(1)} %get-tuple-element.31), channel_id=1, source_target_pairs={{16,0},{32,16},{48,32},{64,48},{80,64},{96,80},{112,96},{17,1},{33... | collective-permute-start | bytes 786440 | tf_op jit(solution)/shard_map/ppermute | solution.py:17
  24.3 16.4 %collective-permute-start.3 = (f32[32,1,16,128]{3,0,2,1:T(8,128)S(1)}, f32[32,1,16,128]{3,0,2,1:T(8,128)S(1)}, u32[]{:S(2)}, u32[]{:S(2)}) collective-permute-start(f32[32,1,16,128]{3,0,2,1:T(8,128)S(1)} %get-tuple-element.33), channel_id=1, source_target_pairs={{0,16},{16,32},{32,48},{48,64},{64,80},{80,96},{96,112},{1,17},{17... | collective-permute-start | bytes 786440 | tf_op jit(solution)/shard_map/ppermute | solution.py:14
  26.2 19.6 %collective-permute-start.1 = (f32[32,1,16,128]{3,0,2,1:T(8,128)S(1)}, f32[32,1,16,128]{3,0,2,1:T(8,128)S(1)}, u32[]{:S(2)}, u32[]{:S(2)}) collective-permute-start(f32[32,1,16,128]{3,0,2,1:T(8,128)S(1)} %get-tuple-element.32), channel_id=1, source_target_pairs={{16,0},{32,16},{48,32},{64,48},{80,64},{96,80},{112,96},{17,1},{33... | collective-permute-start | bytes 786440 | tf_op jit(solution)/shard_map/ppermute | solution.py:17
  36.3 16.9 %collective-permute-start.4 = (f32[32,18,1,128]{3,0,2,1:T(8,128)S(1)}, f32[32,18,1,128]{3,0,2,1:T(8,128)S(1)}, u32[]{:S(2)}, u32[]{:S(2)}) collective-permute-start(f32[32,18,1,128]{3,0,2,1:T(8,128)S(1)} %get-tuple-element.21), channel_id=1, source_target_pairs={{2,0},{4,2},{6,4},{8,6},{10,8},{12,10},{14,12},{3,1},{5,3},{7,5},{... | collective-permute-start | bytes 884744 | tf_op jit(solution)/shard_map/ppermute | solution.py:17
  37.6 15.6 %collective-permute-start.6 = (f32[32,18,1,128]{3,0,2,1:T(8,128)S(1)}, f32[32,18,1,128]{3,0,2,1:T(8,128)S(1)}, u32[]{:S(2)}, u32[]{:S(2)}) collective-permute-start(f32[32,18,1,128]{3,0,2,1:T(8,128)S(1)} %get-tuple-element.20), channel_id=1, source_target_pairs={{0,2},{2,4},{4,6},{6,8},{8,10},{10,12},{12,14},{1,3},{3,5},{5,7},{... | collective-permute-start | bytes 884744 | tf_op jit(solution)/shard_map/ppermute | solution.py:14
  47.6 5.6 %collective-permute-start.5 = (f32[32,18,1,128]{3,0,2,1:T(8,128)S(1)}, f32[32,18,1,128]{3,0,2,1:T(8,128)S(1)}, u32[]{:S(2)}, u32[]{:S(2)}) collective-permute-start(f32[32,18,1,128]{3,0,2,1:T(8,128)S(1)} %get-tuple-element.22), channel_id=1, source_target_pairs={{2,0},{4,2},{6,4},{8,6},{10,8},{12,10},{14,12},{3,1},{5,3},{7,5},{... | collective-permute-start | bytes 884744 | tf_op jit(solution)/shard_map/ppermute | solution.py:17
  48.9 5.3 collective-permute-start.7
  64.5 8.3 %collective-permute-start.8 = (f32[32,1,16,128]{3,0,2,1:T(8,128)S(1)}, f32[32,1,16,128]{3,0,2,1:T(8,128)S(1)}, u32[]{:S(2)}, u32[]{:S(2)}) collective-permute-start(f32[32,1,16,128]{3,0,2,1:T(8,128)S(1)} %get-tuple-element.29), channel_id=1, source_target_pairs={{16,0},{32,16},{48,32},{64,48},{80,64},{96,80},{112,96},{17,1},{33... | collective-permute-start | bytes 786440 | tf_op jit(solution)/shard_map/ppermute | solution.py:17
  66.5 11.9 %collective-permute-start.9 = (f32[32,1,16,128]{3,0,2,1:T(8,128)S(1)}, f32[32,1,16,128]{3,0,2,1:T(8,128)S(1)}, u32[]{:S(2)}, u32[]{:S(2)}) collective-permute-start(f32[32,1,16,128]{3,0,2,1:T(8,128)S(1)} %get-tuple-element.28), channel_id=1, source_target_pairs={{0,16},{16,32},{32,48},{48,64},{64,80},{80,96},{96,112},{1,17},{17... | collective-permute-start | bytes 786440 | tf_op jit(solution)/shard_map/ppermute | solution.py:14
  78.4 6.9 %collective-permute-start.10 = (f32[32,18,1,128]{3,0,2,1:T(8,128)S(1)}, f32[32,18,1,128]{3,0,2,1:T(8,128)S(1)}, u32[]{:S(2)}, u32[]{:S(2)}) collective-permute-start(f32[32,18,1,128]{3,0,2,1:T(8,128)S(1)} %get-tuple-element.18), channel_id=1, source_target_pairs={{2,0},{4,2},{6,4},{8,6},{10,8},{12,10},{14,12},{3,1},{5,3},{7,5},{... | collective-permute-start | bytes 884744 | tf_op jit(solution)/shard_map/ppermute | solution.py:17
  79.7 6.8 %collective-permute-start.11 = (f32[32,18,1,128]{3,0,2,1:T(8,128)S(1)}, f32[32,18,1,128]{3,0,2,1:T(8,128)S(1)}, u32[]{:S(2)}, u32[]{:S(2)}) collective-permute-start(f32[32,18,1,128]{3,0,2,1:T(8,128)S(1)} %get-tuple-element.19), channel_id=1, source_target_pairs={{0,2},{2,4},{4,6},{6,8},{8,10},{10,12},{12,14},{1,3},{3,5},{5,7},{... | collective-permute-start | bytes 884744 | tf_op jit(solution)/shard_map/ppermute | solution.py:14
  94.6 8.3 %collective-permute-start.12 = (f32[32,1,16,128]{3,0,2,1:T(8,128)S(1)}, f32[32,1,16,128]{3,0,2,1:T(8,128)S(1)}, u32[]{:S(2)}, u32[]{:S(2)}) collective-permute-start(f32[32,1,16,128]{3,0,2,1:T(8,128)S(1)} %get-tuple-element.27), channel_id=1, source_target_pairs={{16,0},{32,16},{48,32},{64,48},{80,64},{96,80},{112,96},{17,1},{33... | collective-permute-start | bytes 786440 | tf_op jit(solution)/shard_map/ppermute | solution.py:17
  96.5 11.9 %collective-permute-start.13 = (f32[32,1,16,128]{3,0,2,1:T(8,128)S(1)}, f32[32,1,16,128]{3,0,2,1:T(8,128)S(1)}, u32[]{:S(2)}, u32[]{:S(2)}) collective-permute-start(f32[32,1,16,128]{3,0,2,1:T(8,128)S(1)} %get-tuple-element.26), channel_id=1, source_target_pairs={{0,16},{16,32},{32,48},{48,64},{64,80},{80,96},{96,112},{1,17},{17... | collective-permute-start | bytes 786440 | tf_op jit(solution)/shard_map/ppermute | solution.py:14
  108.5 10.2 %collective-permute-start.14 = (f32[32,18,1,128]{3,0,2,1:T(8,128)S(1)}, f32[32,18,1,128]{3,0,2,1:T(8,128)S(1)}, u32[]{:S(2)}, u32[]{:S(2)}) collective-permute-start(f32[32,18,1,128]{3,0,2,1:T(8,128)S(1)} %get-tuple-element.16), channel_id=1, source_target_pairs={{2,0},{4,2},{6,4},{8,6},{10,8},{12,10},{14,12},{3,1},{5,3},{7,5},{... | collective-permute-start | bytes 884744 | tf_op jit(solution)/shard_map/ppermute | solution.py:17
  109.8 10.1 %collective-permute-start.15 = (f32[32,18,1,128]{3,0,2,1:T(8,128)S(1)}, f32[32,18,1,128]{3,0,2,1:T(8,128)S(1)}, u32[]{:S(2)}, u32[]{:S(2)}) collective-permute-start(f32[32,18,1,128]{3,0,2,1:T(8,128)S(1)} %get-tuple-element.17), channel_id=1, source_target_pairs={{0,2},{2,4},{4,6},{6,8},{8,10},{10,12},{12,14},{1,3},{3,5},{5,7},{... | collective-permute-start | bytes 884744 | tf_op jit(solution)/shard_map/ppermute | solution.py:14
  128.0 8.3 %collective-permute-start.16 = (f32[32,1,16,128]{3,0,2,1:T(8,128)S(1)}, f32[32,1,16,128]{3,0,2,1:T(8,128)S(1)}, u32[]{:S(2)}, u32[]{:S(2)}) collective-permute-start(f32[32,1,16,128]{3,0,2,1:T(8,128)S(1)} %get-tuple-element.25), channel_id=1, source_target_pairs={{16,0},{32,16},{48,32},{64,48},{80,64},{96,80},{112,96},{17,1},{33... | collective-permute-start | bytes 786440 | tf_op jit(solution)/shard_map/ppermute | solution.py:17
  129.9 11.9 %collective-permute-start.17 = (f32[32,1,16,128]{3,0,2,1:T(8,128)S(1)}, f32[32,1,16,128]{3,0,2,1:T(8,128)S(1)}, u32[]{:S(2)}, u32[]{:S(2)}) collective-permute-start(f32[32,1,16,128]{3,0,2,1:T(8,128)S(1)} %get-tuple-element.24), channel_id=1, source_target_pairs={{0,16},{16,32},{32,48},{48,64},{64,80},{80,96},{96,112},{1,17},{17... | collective-permute-start | bytes 786440 | tf_op jit(solution)/shard_map/ppermute | solution.py:14
  141.8 9.9 %collective-permute-start.18 = (f32[32,18,1,128]{3,0,2,1:T(8,128)S(1)}, f32[32,18,1,128]{3,0,2,1:T(8,128)S(1)}, u32[]{:S(2)}, u32[]{:S(2)}) collective-permute-start(f32[32,18,1,128]{3,0,2,1:T(8,128)S(1)} %get-tuple-element.14), channel_id=1, source_target_pairs={{2,0},{4,2},{6,4},{8,6},{10,8},{12,10},{14,12},{3,1},{5,3},{7,5},{... | collective-permute-start | bytes 884744 | tf_op jit(solution)/shard_map/ppermute | solution.py:17
  143.1 9.8 %collective-permute-start.19 = (f32[32,18,1,128]{3,0,2,1:T(8,128)S(1)}, f32[32,18,1,128]{3,0,2,1:T(8,128)S(1)}, u32[]{:S(2)}, u32[]{:S(2)}) collective-permute-start(f32[32,18,1,128]{3,0,2,1:T(8,128)S(1)} %get-tuple-element.15), channel_id=1, source_target_pairs={{0,2},{2,4},{4,6},{6,8},{8,10},{10,12},{12,14},{1,3},{3,5},{5,7},{... | collective-permute-start | bytes 884744 | tf_op jit(solution)/shard_map/ppermute | solution.py:14
  164.8 6.8 %copy-start.5 = (bf16[64,16,16,128]{3,2,1,0:T(8,128)(2,1)S(1)}, bf16[64,16,16,128]{3,2,1,0:T(8,128)(2,1)}, u32[]{:S(2)}) copy-start(bf16[64,16,16,128]{3,2,1,0:T(8,128)(2,1)} %param.9) | copy-start | bytes 12582916
  171.6 334.0 %copy-start.4 = (f32[64,32]{0,1:T(8,128)S(1)}, f32[64,32]{0,1:T(8,128)}, u32[]{:S(2)}) copy-start(f32[64,32]{0,1:T(8,128)} %param.11) | copy-start | bytes 24580
  511.1 1.6 copy-start.3
Sparse Core Ops, SparseCore 0:
  164.9 63.2 all-gather.1
where the time goes:
time: 527 us; the launch traced here: 526 us
  blocking collectives  330 us (63%)
  starting transfers between devices  73.6 us (14%)
  other arithmetic  36.9 us (7%)
  local copies, waits for them, and re-layouts  34.4 us (7%)
  waiting for transfers between devices  28.3 us (5%)
  between operations  14.5 us (3%)
  matrix products  7.84 us (1%)
    psum x1, blocking collectives, per_device(): corange_sketch = corange_prev + lax.psum(partial_value, ('sx', 'sy'))  330 us
    ppermute x10, starting transfers between devices, extended(): lax.ppermute(lax.slice_in_dim(block, block.shape[dim] - width, None, axis...  47.4 us
    unnamed x22, local copies, waits for them, and re-layouts  30.2 us
    add x3, other arithmetic, advance(): return center + 0.16 * total  26.5 us
    ppermute x10, starting transfers between devices, extended(): lax.ppermute(lax.slice_in_dim(block, 0, width, axis=dim), axis, backward)  26.1 us
    ppermute x10, waiting for transfers between devices, extended(): lax.ppermute(lax.slice_in_dim(block, block.shape[dim] - width, None, axis...  21.1 us
  transfers between devices with their start and end apart: 21, of which 10 were waited for; matrix products, arithmetic and copies ran while one was open for 4% of the time, Pallas kernels for 0%

commit v1 on v0

--- a/solution.py
+++ b/solution.py
@@ -68,7 +68,7 @@
     partial_value = lax.dot_general(
         flat_psi, flat_snap, (((1,), (1,)), ((), ())), preferred_element_type=jnp.float32
     )
-    corange_sketch = corange_prev + lax.psum(partial_value, ("sx", "sy"))
+    corange_sketch = corange_prev + jnp.sum(lax.all_gather(partial_value, ("sx", "sy")), axis=0)
     return (state, range_sketch, corange_sketch)
 
 

time: 527 us -> 297 us (0.56)
  blocking collectives: 330 us -> 100 us
    psum x1 -> x0, blocking collectives: 330 us -> none  [per_device(): corange_sketch = corange_prev + lax.psum(partial_value, ('sx', 'sy'))]
    all_gather x0 -> x1, blocking collectives: none -> 100 us  [per_device(): lax.all_gather(partial_value, ('sx', 'sy'))]
  transfers between devices with their start and end apart: 21 -> 21, of which waited for: 10 -> 10; matrix products, arithmetic and copies ran while one was open for 4% -> 8% of each run, Pallas kernels for 0% -> 0%
where the time goes in v1:
time: 297 us; the launch traced here: 296 us
  blocking collectives  100 us (34%)
  starting transfers between devices  73.6 us (25%)
  other arithmetic  37 us (12%)
  local copies, waits for them, and re-layouts  34.4 us (12%)
  waiting for transfers between devices  28.3 us (10%)
  between operations  14.5 us (5%)
  matrix products  7.84 us (3%)
    all_gather x1, blocking collectives, per_device(): lax.all_gather(partial_value, ('sx', 'sy'))  100 us
    ppermute x10, starting transfers between devices, extended(): lax.ppermute(lax.slice_in_dim(block, block.shape[dim] - width, None, axis...  47.4 us
    unnamed x22, local copies, waits for them, and re-layouts  30.2 us
    add x3, other arithmetic, advance(): return center + 0.16 * total  26.5 us
    ppermute x10, starting transfers between devices, extended(): lax.ppermute(lax.slice_in_dim(block, 0, width, axis=dim), axis, backward)  26.1 us
    ppermute x10, waiting for transfers between devices, extended(): lax.ppermute(lax.slice_in_dim(block, block.shape[dim] - width, None, axis...  21.1 us
    convert_element_type x1, other arithmetic, per_device(): snapshot = state.astype(jnp.bfloat16)  9.73 us
    ppermute x10, waiting for transfers between devices, extended(): lax.ppermute(lax.slice_in_dim(block, 0, width, axis=dim), axis, backward)  7.24 us
  transfers between devices with their start and end apart: 21, of which 10 were waited for; matrix products, arithmetic and copies ran while one was open for 8% of the time, Pallas kernels for 0%

profile of v1, /device:TPU:24, one launch (start us, length us, event | category | flops | bytes accessed | tf_op | source)
XLA Modules:
  0.0 296.1 jit_solution(2510224462174614220)
XLA Ops:
  7.2 4.8 %copy.22 = f32[32,16,16,128]{3,0,2,1:T(8,128)S(1)} copy(f32[32,16,16,128]{3,2,1,0:T(8,128)} %param.7) | data formatting | bytes 8388608 | tf_op args[1]
  12.0 3.4 %collective-permute-start.2 = (f32[32,1,16,128]{3,0,2,1:T(8,128)S(1)}, f32[32,1,16,128]{3,0,2,1:T(8,128)S(1)}, u32[]{:S(2)}, u32[]{:S(2)}) collective-permute-start(f32[32,1,16,128]{3,0,2,1:T(8,128)S(1)} %get-tuple-element.30), channel_id=1, source_target_pairs={{0,16},{16,32},{32,48},{48,64},{64,80},{80,96},{96,112},{1,17},{17... | collective-permute-start | bytes 786440 | tf_op jit(solution)/shard_map/ppermute | solution.py:14
  15.5 6.3 %collective-permute-start = (f32[32,1,16,128]{3,0,2,1:T(8,128)S(1)}, f32[32,1,16,128]{3,0,2,1:T(8,128)S(1)}, u32[]{:S(2)}, u32[]{:S(2)}) collective-permute-start(f32[32,1,16,128]{3,0,2,1:T(8,128)S(1)} %get-tuple-element.31), channel_id=1, source_target_pairs={{16,0},{32,16},{48,32},{64,48},{80,64},{96,80},{112,96},{17,1},{33... | collective-permute-start | bytes 786440 | tf_op jit(solution)/shard_map/ppermute | solution.py:17
  21.8 2.4 copy.44
  24.3 1.9 collective-permute-start.3
  26.2 7.5 %collective-permute-start.1 = (f32[32,1,16,128]{3,0,2,1:T(8,128)S(1)}, f32[32,1,16,128]{3,0,2,1:T(8,128)S(1)}, u32[]{:S(2)}, u32[]{:S(2)}) collective-permute-start(f32[32,1,16,128]{3,0,2,1:T(8,128)S(1)} %get-tuple-element.32), channel_id=1, source_target_pairs={{16,0},{32,16},{48,32},{64,48},{80,64},{96,80},{112,96},{17,1},{33... | collective-permute-start | bytes 786440 | tf_op jit(solution)/shard_map/ppermute | solution.py:17
  33.8 2.4 constant_dynamic-update-slice_fusion.1
  36.3 1.3 collective-permute-start.4
  37.6 3.0 %collective-permute-start.6 = (f32[32,18,1,128]{3,0,2,1:T(8,128)S(1)}, f32[32,18,1,128]{3,0,2,1:T(8,128)S(1)}, u32[]{:S(2)}, u32[]{:S(2)}) collective-permute-start(f32[32,18,1,128]{3,0,2,1:T(8,128)S(1)} %get-tuple-element.20), channel_id=1, source_target_pairs={{0,2},{2,4},{4,6},{6,8},{8,10},{10,12},{12,14},{1,3},{3,5},{5,7},{... | collective-permute-start | bytes 884744 | tf_op jit(solution)/shard_map/ppermute | solution.py:14
  41.4 4.4 %constant_dynamic-update-slice_fusion.4 = f32[32,18,16,128]{3,0,2,1:T(8,128)} fusion(f32[32,18,16,128]{3,0,2,1:T(8,128)} %constant_dynamic-update-slice_fusion.5, f32[32,16,16,128]{3,2,1,0:T(8,128)S(1)} %copy-done.2), kind=kLoop, calls=%fused_computation.152 | loop fusion | bytes 8388608
  45.8 0.7 constant_dynamic-update-slice_fusion.3
  46.5 1.1 fusion.103
  47.6 1.3 collective-permute-start.5
  48.9 4.3 %collective-permute-start.7 = (f32[32,18,1,128]{3,0,2,1:T(8,128)S(1)}, f32[32,18,1,128]{3,0,2,1:T(8,128)S(1)}, u32[]{:S(2)}, u32[]{:S(2)}) collective-permute-start(f32[32,18,1,128]{3,0,2,1:T(8,128)S(1)} %get-tuple-element.23), channel_id=1, source_target_pairs={{0,2},{2,4},{4,6},{6,8},{8,10},{10,12},{12,14},{1,3},{3,5},{5,7},{... | collective-permute-start | bytes 884744 | tf_op jit(solution)/shard_map/ppermute | solution.py:14
  53.2 1.0 collective-permute-done.7
  54.2 10.3 %fusion.9 = f32[32,16,16,128]{3,0,2,1:T(8,128)S(1)} fusion(f32[32,16,16,128]{3,0,2,1:T(8,128)S(1)} %copy.44, f32[32,18,16,128]{3,0,2,1:T(8,128)} %constant_dynamic-update-slice_fusion.3, f32[32,18,1,128]{3,0,2,1:T(8,128)S(1)} %collective-permute-done.7, f32[32,18,1,128]{3,0,2,1:T(8,128)S(1)} %collective-permute-done.5, ...), kind=kLoop, calls=%fused_computation.19 | loop fusion | flops 40894464 | bytes 24248320 | tf_op jit(solution)/shard_map/add | solution.py:41
  64.5 1.9 collective-permute-start.8
  66.5 3.9 %collective-permute-start.9 = (f32[32,1,16,128]{3,0,2,1:T(8,128)S(1)}, f32[32,1,16,128]{3,0,2,1:T(8,128)S(1)}, u32[]{:S(2)}, u32[]{:S(2)}) collective-permute-start(f32[32,1,16,128]{3,0,2,1:T(8,128)S(1)} %get-tuple-element.28), channel_id=1, source_target_pairs={{0,16},{16,32},{32,48},{48,64},{64,80},{80,96},{96,112},{1,17},{17... | collective-permute-start | bytes 786440 | tf_op jit(solution)/shard_map/ppermute | solution.py:14
  70.4 2.4 collective-permute-done.8
  72.8 5.5 %collective-permute-done.9 = f32[32,1,16,128]{3,0,2,1:T(8,128)S(1)} collective-permute-done((f32[32,1,16,128]{3,0,2,1:T(8,128)S(1)}, f32[32,1,16,128]{3,0,2,1:T(8,128)S(1)}, u32[]{:S(2)}, u32[]{:S(2)}) %collective-permute-start.9) | collective-permute-done | bytes 262176 | tf_op jit(solution)/shard_map/ppermute | solution.py:14
  78.4 1.3 collective-permute-start.10
  79.7 5.6 %collective-permute-start.11 = (f32[32,18,1,128]{3,0,2,1:T(8,128)S(1)}, f32[32,18,1,128]{3,0,2,1:T(8,128)S(1)}, u32[]{:S(2)}, u32[]{:S(2)}) collective-permute-start(f32[32,18,1,128]{3,0,2,1:T(8,128)S(1)} %get-tuple-element.19), channel_id=1, source_target_pairs={{0,2},{2,4},{4,6},{6,8},{8,10},{10,12},{12,14},{1,3},{3,5},{5,7},{... | collective-permute-start | bytes 884744 | tf_op jit(solution)/shard_map/ppermute | solution.py:14
  85.3 1.2 collective-permute-done.11
  86.5 8.1 %fusion.17 = f32[32,16,16,128]{3,0,2,1:T(8,128)S(1)} fusion(f32[32,16,16,128]{3,0,2,1:T(8,128)S(1)} %fusion.9, f32[32,18,1,128]{3,0,2,1:T(8,128)S(1)} %collective-permute-done.11, f32[32,1,16,128]{3,0,2,1:T(8,128)S(1)} %collective-permute-done.8, f32[32,1,16,128]{3,0,2,1:T(8,128)S(1)} %collective-permute-done.9, ...), kind=kLoop, calls=%fused_computation.27 | loop fusion | flops 45088768 | bytes 19529728 | tf_op jit(solution)/shard_map/add | solution.py:41
  94.6 1.9 collective-permute-start.12
  96.5 3.9 %collective-permute-start.13 = (f32[32,1,16,128]{3,0,2,1:T(8,128)S(1)}, f32[32,1,16,128]{3,0,2,1:T(8,128)S(1)}, u32[]{:S(2)}, u32[]{:S(2)}) collective-permute-start(f32[32,1,16,128]{3,0,2,1:T(8,128)S(1)} %get-tuple-element.26), channel_id=1, source_target_pairs={{0,16},{16,32},{32,48},{48,64},{64,80},{80,96},{96,112},{1,17},{17... | collective-permute-start | bytes 786440 | tf_op jit(solution)/shard_map/ppermute | solution.py:14
  100.5 2.4 collective-permute-done.12
  102.9 5.5 %collective-permute-done.13 = f32[32,1,16,128]{3,0,2,1:T(8,128)S(1)} collective-permute-done((f32[32,1,16,128]{3,0,2,1:T(8,128)S(1)}, f32[32,1,16,128]{3,0,2,1:T(8,128)S(1)}, u32[]{:S(2)}, u32[]{:S(2)}) %collective-permute-start.13) | collective-permute-done | bytes 262176 | tf_op jit(solution)/shard_map/ppermute | solution.py:14
  108.5 1.3 collective-permute-start.14
  109.8 8.9 %collective-permute-start.15 = (f32[32,18,1,128]{3,0,2,1:T(8,128)S(1)}, f32[32,18,1,128]{3,0,2,1:T(8,128)S(1)}, u32[]{:S(2)}, u32[]{:S(2)}) collective-permute-start(f32[32,18,1,128]{3,0,2,1:T(8,128)S(1)} %get-tuple-element.17), channel_id=1, source_target_pairs={{0,2},{2,4},{4,6},{6,8},{8,10},{10,12},{12,14},{1,3},{3,5},{5,7},{... | collective-permute-start | bytes 884744 | tf_op jit(solution)/shard_map/ppermute | solution.py:14
  118.7 1.2 collective-permute-done.15
  119.8 8.1 %fusion.25 = f32[32,16,16,128]{3,0,2,1:T(8,128)S(1)} fusion(f32[32,16,16,128]{3,0,2,1:T(8,128)S(1)} %fusion.17, f32[32,18,1,128]{3,0,2,1:T(8,128)S(1)} %collective-permute-done.15, f32[32,1,16,128]{3,0,2,1:T(8,128)S(1)} %collective-permute-done.12, f32[32,1,16,128]{3,0,2,1:T(8,128)S(1)} %collective-permute-done.13, ...), kind=kLoop, calls=%fused_computation.35 | loop fusion | flops 45088768 | bytes 19529728 | tf_op jit(solution)/shard_map/add | solution.py:41
  128.0 1.9 collective-permute-start.16
  129.9 3.9 %collective-permute-start.17 = (f32[32,1,16,128]{3,0,2,1:T(8,128)S(1)}, f32[32,1,16,128]{3,0,2,1:T(8,128)S(1)}, u32[]{:S(2)}, u32[]{:S(2)}) collective-permute-start(f32[32,1,16,128]{3,0,2,1:T(8,128)S(1)} %get-tuple-element.24), channel_id=1, source_target_pairs={{0,16},{16,32},{32,48},{48,64},{64,80},{80,96},{96,112},{1,17},{17... | collective-permute-start | bytes 786440 | tf_op jit(solution)/shard_map/ppermute | solution.py:14
  133.8 2.4 collective-permute-done.16
  136.2 5.5 %collective-permute-done.17 = f32[32,1,16,128]{3,0,2,1:T(8,128)S(1)} collective-permute-done((f32[32,1,16,128]{3,0,2,1:T(8,128)S(1)}, f32[32,1,16,128]{3,0,2,1:T(8,128)S(1)}, u32[]{:S(2)}, u32[]{:S(2)}) %collective-permute-start.17) | collective-permute-done | bytes 262176 | tf_op jit(solution)/shard_map/ppermute | solution.py:14
  141.8 1.3 collective-permute-start.18
  143.1 8.6 %collective-permute-start.19 = (f32[32,18,1,128]{3,0,2,1:T(8,128)S(1)}, f32[32,18,1,128]{3,0,2,1:T(8,128)S(1)}, u32[]{:S(2)}, u32[]{:S(2)}) collective-permute-start(f32[32,18,1,128]{3,0,2,1:T(8,128)S(1)} %get-tuple-element.15), channel_id=1, source_target_pairs={{0,2},{2,4},{4,6},{6,8},{8,10},{10,12},{12,14},{1,3},{3,5},{5,7},{... | collective-permute-start | bytes 884744 | tf_op jit(solution)/shard_map/ppermute | solution.py:14
  151.7 1.2 collective-permute-done.19
  152.9 9.7 %fusion.100 = (bf16[32,16,16,128]{3,0,2,1:T(8,128)(2,1)S(1)}, f32[32,16,16,128]{3,0,2,1:T(8,128)}) fusion(f32[32,16,16,128]{3,0,2,1:T(8,128)S(1)} %fusion.25, f32[32,16,16,128]{3,0,2,1:T(8,128)S(1)} %copy.22, f32[32,1,16,128]{3,0,2,1:T(8,128)S(1)} %collective-permute-done.16, f32[32,1,16,128]{3,0,2,1:T(8,128)S(1)} %collective-permute-done.17, ...), kind=kLoop, calls=%fused_computation.155 | loop fusion | flops 46137344 | bytes 21626880 | tf_op jit(solution)/shard_map/convert_element_type | solution.py:51
  162.6 2.1 copy.47
  164.8 6.8 %copy.50 = f32[32,16,16,128]{3,2,1,0:T(8,128)} copy(f32[32,16,16,128]{3,0,2,1:T(8,128)} %get-tuple-element.13) | data formatting | bytes 8388608
  171.6 3.7 %fusion.94 = f32[1,64,32]{1,2,0:T(8,128)S(1)} fusion(bf16[32,16,16,128]{3,0,2,1:T(8,128)(2,1)S(1)} %get-tuple-element.12, bf16[64,16,16,128]{3,2,1,0:T(8,128)(2,1)S(1)} %copy-done.5), kind=kOutput, calls=%fused_computation.136 | convolution fusion | flops 134217728 | bytes 6299648 | tf_op jit(solution)/shard_map/dot_general | solution.py:68
  175.3 100.5 %all-gather.1 = f32[64,64,32]{1,2,0:T(8,128)S(1)} all-gather(f32[1,64,32]{1,2,0:T(8,128)S(1)} %fusion.94), channel_id=2, replica_groups=mesh['sx'=8,'sy'=8,'par'=2] {'sx','sy'}, dimensions={0}, use_global_device_ids=true | all-gather | bytes 532480 | tf_op jit(solution)/shard_map/all_gather | solution.py:71
  276.5 4.9 %copy.69 = bf16[8,8,256,128]{3,1,2,0:T(8,128)(2,1)S(1)} copy(bf16[8,8,256,128]{3,2,1,0:T(8,128)(2,1)} %bitcast.29) | data formatting | bytes 8388608
  281.4 1.2 copy.56
  283.0 4.1 %add_convert_fusion = bf16[32,16,16,128]{3,0,2,1:T(8,128)(2,1)S(1)} fusion(bf16[16,16,128,64]{2,1,0,3:T(8,128)(2,1)S(1)} %bitcast.28, bf16[32,16,16,128]{3,2,1,0:T(8,128)(2,1)S(1)} %copy-done.3, bf16[64,64]{1,0:T(8,128)(2,1)S(1)} %copy-done, s32[]{:T(128)S(6)} %select_n.3), kind=kOutput, calls=%fused_computation.135 | convolution fusion | flops 137363456 | bytes 8396804 | tf_op jit(solution)/shard_map/dot_general | solution.py:59
  287.1 2.1 copy.51
  (39 shorter events, 2.3 us)
Async XLA Ops:
  7.2 275.4 %copy-start = (bf16[64,64]{1,0:T(8,128)(2,1)S(1)}, bf16[64,64]{1,0:T(8,128)(2,1)}, u32[]{:S(2)}) copy-start(bf16[64,64]{1,0:T(8,128)(2,1)} %param.8) | copy-start | bytes 24580
  7.2 269.3 %all-gather.4.cloned.1.call-start = ((), (), s32[]{:S(2)}) async-start(), calls=%async_computation | async-start | bytes 6291456 | tf_op jit(solution)/shard_map/all_gather | solution.py:57
  7.2 14.6 %copy-start.2 = (f32[32,16,16,128]{3,2,1,0:T(8,128)S(1)}, f32[32,16,16,128]{3,2,1,0:T(8,128)}, u32[]{:S(2)}) copy-start(f32[32,16,16,128]{3,2,1,0:T(8,128)} %param.6) | copy-start | bytes 12582916
  12.0 21.7 %collective-permute-start.2 = (f32[32,1,16,128]{3,0,2,1:T(8,128)S(1)}, f32[32,1,16,128]{3,0,2,1:T(8,128)S(1)}, u32[]{:S(2)}, u32[]{:S(2)}) collective-permute-start(f32[32,1,16,128]{3,0,2,1:T(8,128)S(1)} %get-tuple-element.30), channel_id=1, source_target_pairs={{0,16},{16,32},{32,48},{48,64},{64,80},{80,96},{96,112},{1,17},{17... | collective-permute-start | bytes 786440 | tf_op jit(solution)/shard_map/ppermute | solution.py:14
  15.5 18.3 %copy-start.1 = (f32[32,16,16,128]{3,2,1,0:T(8,128)S(1)}, f32[32,16,16,128]{3,2,1,0:T(8,128)}, u32[]{:S(2)}) copy-start(f32[32,16,16,128]{3,2,1,0:T(8,128)} %param.7) | copy-start | bytes 12582916
  15.5 20.8 %collective-permute-start = (f32[32,1,16,128]{3,0,2,1:T(8,128)S(1)}, f32[32,1,16,128]{3,0,2,1:T(8,128)S(1)}, u32[]{:S(2)}, u32[]{:S(2)}) collective-permute-start(f32[32,1,16,128]{3,0,2,1:T(8,128)S(1)} %get-tuple-element.31), channel_id=1, source_target_pairs={{16,0},{32,16},{48,32},{64,48},{80,64},{96,80},{112,96},{17,1},{33... | collective-permute-start | bytes 786440 | tf_op jit(solution)/shard_map/ppermute | solution.py:17
  24.3 16.4 %collective-permute-start.3 = (f32[32,1,16,128]{3,0,2,1:T(8,128)S(1)}, f32[32,1,16,128]{3,0,2,1:T(8,128)S(1)}, u32[]{:S(2)}, u32[]{:S(2)}) collective-permute-start(f32[32,1,16,128]{3,0,2,1:T(8,128)S(1)} %get-tuple-element.33), channel_id=1, source_target_pairs={{0,16},{16,32},{32,48},{48,64},{64,80},{80,96},{96,112},{1,17},{17... | collective-permute-start | bytes 786440 | tf_op jit(solution)/shard_map/ppermute | solution.py:14
  26.2 19.6 %collective-permute-start.1 = (f32[32,1,16,128]{3,0,2,1:T(8,128)S(1)}, f32[32,1,16,128]{3,0,2,1:T(8,128)S(1)}, u32[]{:S(2)}, u32[]{:S(2)}) collective-permute-start(f32[32,1,16,128]{3,0,2,1:T(8,128)S(1)} %get-tuple-element.32), channel_id=1, source_target_pairs={{16,0},{32,16},{48,32},{64,48},{80,64},{96,80},{112,96},{17,1},{33... | collective-permute-start | bytes 786440 | tf_op jit(solution)/shard_map/ppermute | solution.py:17
  36.3 16.9 %collective-permute-start.4 = (f32[32,18,1,128]{3,0,2,1:T(8,128)S(1)}, f32[32,18,1,128]{3,0,2,1:T(8,128)S(1)}, u32[]{:S(2)}, u32[]{:S(2)}) collective-permute-start(f32[32,18,1,128]{3,0,2,1:T(8,128)S(1)} %get-tuple-element.21), channel_id=1, source_target_pairs={{2,0},{4,2},{6,4},{8,6},{10,8},{12,10},{14,12},{3,1},{5,3},{7,5},{... | collective-permute-start | bytes 884744 | tf_op jit(solution)/shard_map/ppermute | solution.py:17
  37.6 15.6 %collective-permute-start.6 = (f32[32,18,1,128]{3,0,2,1:T(8,128)S(1)}, f32[32,18,1,128]{3,0,2,1:T(8,128)S(1)}, u32[]{:S(2)}, u32[]{:S(2)}) collective-permute-start(f32[32,18,1,128]{3,0,2,1:T(8,128)S(1)} %get-tuple-element.20), channel_id=1, source_target_pairs={{0,2},{2,4},{4,6},{6,8},{8,10},{10,12},{12,14},{1,3},{3,5},{5,7},{... | collective-permute-start | bytes 884744 | tf_op jit(solution)/shard_map/ppermute | solution.py:14
  47.6 5.6 %collective-permute-start.5 = (f32[32,18,1,128]{3,0,2,1:T(8,128)S(1)}, f32[32,18,1,128]{3,0,2,1:T(8,128)S(1)}, u32[]{:S(2)}, u32[]{:S(2)}) collective-permute-start(f32[32,18,1,128]{3,0,2,1:T(8,128)S(1)} %get-tuple-element.22), channel_id=1, source_target_pairs={{2,0},{4,2},{6,4},{8,6},{10,8},{12,10},{14,12},{3,1},{5,3},{7,5},{... | collective-permute-start | bytes 884744 | tf_op jit(solution)/shard_map/ppermute | solution.py:17
  48.9 5.3 %collective-permute-start.7 = (f32[32,18,1,128]{3,0,2,1:T(8,128)S(1)}, f32[32,18,1,128]{3,0,2,1:T(8,128)S(1)}, u32[]{:S(2)}, u32[]{:S(2)}) collective-permute-start(f32[32,18,1,128]{3,0,2,1:T(8,128)S(1)} %get-tuple-element.23), channel_id=1, source_target_pairs={{0,2},{2,4},{4,6},{6,8},{8,10},{10,12},{12,14},{1,3},{3,5},{5,7},{... | collective-permute-start | bytes 884744 | tf_op jit(solution)/shard_map/ppermute | solution.py:14
  64.5 8.3 %collective-permute-start.8 = (f32[32,1,16,128]{3,0,2,1:T(8,128)S(1)}, f32[32,1,16,128]{3,0,2,1:T(8,128)S(1)}, u32[]{:S(2)}, u32[]{:S(2)}) collective-permute-start(f32[32,1,16,128]{3,0,2,1:T(8,128)S(1)} %get-tuple-element.29), channel_id=1, source_target_pairs={{16,0},{32,16},{48,32},{64,48},{80,64},{96,80},{112,96},{17,1},{33... | collective-permute-start | bytes 786440 | tf_op jit(solution)/shard_map/ppermute | solution.py:17
  66.5 11.9 %collective-permute-start.9 = (f32[32,1,16,128]{3,0,2,1:T(8,128)S(1)}, f32[32,1,16,128]{3,0,2,1:T(8,128)S(1)}, u32[]{:S(2)}, u32[]{:S(2)}) collective-permute-start(f32[32,1,16,128]{3,0,2,1:T(8,128)S(1)} %get-tuple-element.28), channel_id=1, source_target_pairs={{0,16},{16,32},{32,48},{48,64},{64,80},{80,96},{96,112},{1,17},{17... | collective-permute-start | bytes 786440 | tf_op jit(solution)/shard_map/ppermute | solution.py:14
  78.4 6.9 %collective-permute-start.10 = (f32[32,18,1,128]{3,0,2,1:T(8,128)S(1)}, f32[32,18,1,128]{3,0,2,1:T(8,128)S(1)}, u32[]{:S(2)}, u32[]{:S(2)}) collective-permute-start(f32[32,18,1,128]{3,0,2,1:T(8,128)S(1)} %get-tuple-element.18), channel_id=1, source_target_pairs={{2,0},{4,2},{6,4},{8,6},{10,8},{12,10},{14,12},{3,1},{5,3},{7,5},{... | collective-permute-start | bytes 884744 | tf_op jit(solution)/shard_map/ppermute | solution.py:17
  79.7 6.8 %collective-permute-start.11 = (f32[32,18,1,128]{3,0,2,1:T(8,128)S(1)}, f32[32,18,1,128]{3,0,2,1:T(8,128)S(1)}, u32[]{:S(2)}, u32[]{:S(2)}) collective-permute-start(f32[32,18,1,128]{3,0,2,1:T(8,128)S(1)} %get-tuple-element.19), channel_id=1, source_target_pairs={{0,2},{2,4},{4,6},{6,8},{8,10},{10,12},{12,14},{1,3},{3,5},{5,7},{... | collective-permute-start | bytes 884744 | tf_op jit(solution)/shard_map/ppermute | solution.py:14
  94.6 8.3 %collective-permute-start.12 = (f32[32,1,16,128]{3,0,2,1:T(8,128)S(1)}, f32[32,1,16,128]{3,0,2,1:T(8,128)S(1)}, u32[]{:S(2)}, u32[]{:S(2)}) collective-permute-start(f32[32,1,16,128]{3,0,2,1:T(8,128)S(1)} %get-tuple-element.27), channel_id=1, source_target_pairs={{16,0},{32,16},{48,32},{64,48},{80,64},{96,80},{112,96},{17,1},{33... | collective-permute-start | bytes 786440 | tf_op jit(solution)/shard_map/ppermute | solution.py:17
  96.5 11.9 %collective-permute-start.13 = (f32[32,1,16,128]{3,0,2,1:T(8,128)S(1)}, f32[32,1,16,128]{3,0,2,1:T(8,128)S(1)}, u32[]{:S(2)}, u32[]{:S(2)}) collective-permute-start(f32[32,1,16,128]{3,0,2,1:T(8,128)S(1)} %get-tuple-element.26), channel_id=1, source_target_pairs={{0,16},{16,32},{32,48},{48,64},{64,80},{80,96},{96,112},{1,17},{17... | collective-permute-start | bytes 786440 | tf_op jit(solution)/shard_map/ppermute | solution.py:14
  108.5 10.2 %collective-permute-start.14 = (f32[32,18,1,128]{3,0,2,1:T(8,128)S(1)}, f32[32,18,1,128]{3,0,2,1:T(8,128)S(1)}, u32[]{:S(2)}, u32[]{:S(2)}) collective-permute-start(f32[32,18,1,128]{3,0,2,1:T(8,128)S(1)} %get-tuple-element.16), channel_id=1, source_target_pairs={{2,0},{4,2},{6,4},{8,6},{10,8},{12,10},{14,12},{3,1},{5,3},{7,5},{... | collective-permute-start | bytes 884744 | tf_op jit(solution)/shard_map/ppermute | solution.py:17
  109.8 10.1 %collective-permute-start.15 = (f32[32,18,1,128]{3,0,2,1:T(8,128)S(1)}, f32[32,18,1,128]{3,0,2,1:T(8,128)S(1)}, u32[]{:S(2)}, u32[]{:S(2)}) collective-permute-start(f32[32,18,1,128]{3,0,2,1:T(8,128)S(1)} %get-tuple-element.17), channel_id=1, source_target_pairs={{0,2},{2,4},{4,6},{6,8},{8,10},{10,12},{12,14},{1,3},{3,5},{5,7},{... | collective-permute-start | bytes 884744 | tf_op jit(solution)/shard_map/ppermute | solution.py:14
  128.0 8.3 %collective-permute-start.16 = (f32[32,1,16,128]{3,0,2,1:T(8,128)S(1)}, f32[32,1,16,128]{3,0,2,1:T(8,128)S(1)}, u32[]{:S(2)}, u32[]{:S(2)}) collective-permute-start(f32[32,1,16,128]{3,0,2,1:T(8,128)S(1)} %get-tuple-element.25), channel_id=1, source_target_pairs={{16,0},{32,16},{48,32},{64,48},{80,64},{96,80},{112,96},{17,1},{33... | collective-permute-start | bytes 786440 | tf_op jit(solution)/shard_map/ppermute | solution.py:17
  129.9 11.9 %collective-permute-start.17 = (f32[32,1,16,128]{3,0,2,1:T(8,128)S(1)}, f32[32,1,16,128]{3,0,2,1:T(8,128)S(1)}, u32[]{:S(2)}, u32[]{:S(2)}) collective-permute-start(f32[32,1,16,128]{3,0,2,1:T(8,128)S(1)} %get-tuple-element.24), channel_id=1, source_target_pairs={{0,16},{16,32},{32,48},{48,64},{64,80},{80,96},{96,112},{1,17},{17... | collective-permute-start | bytes 786440 | tf_op jit(solution)/shard_map/ppermute | solution.py:14
  141.8 9.9 %collective-permute-start.18 = (f32[32,18,1,128]{3,0,2,1:T(8,128)S(1)}, f32[32,18,1,128]{3,0,2,1:T(8,128)S(1)}, u32[]{:S(2)}, u32[]{:S(2)}) collective-permute-start(f32[32,18,1,128]{3,0,2,1:T(8,128)S(1)} %get-tuple-element.14), channel_id=1, source_target_pairs={{2,0},{4,2},{6,4},{8,6},{10,8},{12,10},{14,12},{3,1},{5,3},{7,5},{... | collective-permute-start | bytes 884744 | tf_op jit(solution)/shard_map/ppermute | solution.py:17
  143.1 9.8 %collective-permute-start.19 = (f32[32,18,1,128]{3,0,2,1:T(8,128)S(1)}, f32[32,18,1,128]{3,0,2,1:T(8,128)S(1)}, u32[]{:S(2)}, u32[]{:S(2)}) collective-permute-start(f32[32,18,1,128]{3,0,2,1:T(8,128)S(1)} %get-tuple-element.15), channel_id=1, source_target_pairs={{0,2},{2,4},{4,6},{6,8},{8,10},{10,12},{12,14},{1,3},{3,5},{5,7},{... | collective-permute-start | bytes 884744 | tf_op jit(solution)/shard_map/ppermute | solution.py:14
  164.8 6.8 %copy-start.5 = (bf16[64,16,16,128]{3,2,1,0:T(8,128)(2,1)S(1)}, bf16[64,16,16,128]{3,2,1,0:T(8,128)(2,1)}, u32[]{:S(2)}) copy-start(bf16[64,16,16,128]{3,2,1,0:T(8,128)(2,1)} %param.9) | copy-start | bytes 12582916
  171.6 104.3 %copy-start.4 = (f32[64,32]{0,1:T(8,128)S(1)}, f32[64,32]{0,1:T(8,128)}, u32[]{:S(2)}) copy-start(f32[64,32]{0,1:T(8,128)} %param.11) | copy-start | bytes 24580
  281.4 1.6 copy-start.3
Sparse Core Ops, SparseCore 0:
  164.9 63.2 all-gather.3
